TPU v7x, 32 devices: a whole 2x2x4 slice. The times are simulated.
32 devices in a mesh: dp: 2 (over core), row: 4 (over y, x), col: 4 (over z).
Axes of the slice: x: 2, y: 2, z: 4, core: 2. Of those that a mesh axis runs over, the one named last changes fastest.
Arguments:
- tokens: bfloat16 [8192, 1024], P(('dp', 'row'), 'col'), may hold values from -6 to 6
- segment_ids: int32 [16, 512], P(('dp', 'col')), may hold values from 0 to 7, never falling along the last dimension, each value on 1 to 256 neighbouring positions
- gain_attn: float32 [1024], P('col'), may hold values from 0.5 to 1.5
- gain_ffn: float32 [1024], P('col'), may hold values from 0.5 to 1.5
- w_qkv: bfloat16 [1024, 3, 1024], P('col', None, 'row'), may hold values from -0.1875 to 0.1875
- w_out: bfloat16 [1024, 1024], P('row', 'col'), may hold values from -1 to 1
- w_gate_up: bfloat16 [1024, 2, 2816], P('col', None, 'row'), may hold values from -0.1875 to 0.1875
- w_down: bfloat16 [2816, 1024], P('row', 'col'), may hold values from -0.109375 to 0.109375
- grad_out: bfloat16 [8192, 1024], P(('dp', 'row'), 'col'), may hold values from -6 to 6
Outputs:
- output: bfloat16 [8192, 1024], P(('dp', 'row'), 'col')
- grad_tokens: float32 [8192, 1024], P(('dp', 'row'), 'col')
- grad_gain_attn: float32 [1024], P('col')
- grad_gain_ffn: float32 [1024], P('col')
- grad_w_qkv: float32 [1024, 3, 1024], P('col', None, 'row')
- grad_w_out: float32 [1024, 1024], P('row', 'col')
- grad_w_gate_up: float32 [1024, 2, 2816], P('col', None, 'row')
- grad_w_down: float32 [2816, 1024], P('row', 'col')
Inputs may be any that keep to these rules, and one draw needn't show every extreme that they name: `segment_ids`: in each sequence the ids never fall along its 512 positions; each of the 8 ids covers 1 to 256 consecutive positions.
All inputs are finite; a program needn't handle non-finite values.
Results may differ from a plain program's by a relative error of at most 0.013.
The roundings to bfloat16 on the way count: a program that leaves them out, or rounds other values in their place, can miss the bound.
Values may be sent and summed in bfloat16 or wider, within the bound.
No kernel may reach another device: no remote copies, remote signals or barrier semaphores. Data moves between devices by JAX's collectives and lax.ppermute only.
A program may use at most 256 MiB of HBM per device.

v0:
```python
import jax
import jax.numpy as jnp
from jax import lax
from jax.sharding import PartitionSpec as P

D = 1024
HEAD_DIM = 64


EPS = 1e-06
MASKED = -1e30


def row_norm(values, gain_vec):
    squares = lax.psum(jnp.sum(values * values, axis=1), "col")
    rescale = lax.rsqrt(squares / D + EPS)
    unit_rows = values * rescale[:, None]
    return (unit_rows, rescale, (unit_rows * gain_vec[None, :]).astype(jnp.bfloat16))


def norm_backward(grad_normed, unit_rows, rescale, gain_vec):
    weighted = grad_normed * gain_vec[None, :]
    inner_sum = lax.psum(jnp.sum(weighted * unit_rows, axis=1), "col")
    grad_in = rescale[:, None] * (weighted - unit_rows * (inner_sum / D)[:, None])
    grad_gain = jnp.sum(grad_normed * unit_rows, axis=0)
    return (grad_in, grad_gain)


def project_up(normed, weight_block):
    gathered = lax.all_gather(normed, "row", axis=0, tiled=True)

    def term(begin_at, row_count):
        return jnp.dot(gathered, weight_block, preferred_element_type=jnp.float32)

    result = lax.psum_scatter(
        term(jnp.int32(0), gathered.shape[0] // lax.axis_size("col") * lax.axis_size("col")),
        "col",
        scatter_dimension=0,
        tiled=True,
    )
    return (gathered, result.astype(jnp.bfloat16))


def project_down(values, weight_block):
    gathered = lax.all_gather(values, "col", axis=0, tiled=True)

    def term(begin_at, row_count):
        return jnp.dot(gathered, weight_block, preferred_element_type=jnp.float32)

    result = lax.psum_scatter(
        term(jnp.int32(0), gathered.shape[0] // lax.axis_size("row") * lax.axis_size("row")),
        "row",
        scatter_dimension=0,
        tiled=True,
    )
    return (gathered, result)


def back_down(grad_rows, weight_block):
    gathered = lax.all_gather(grad_rows, "row", axis=0, tiled=True)

    def term(begin_at, row_count):
        return lax.dot_general(
            gathered, weight_block, (((1,), (1,)), ((), ())), preferred_element_type=jnp.float32
        )

    result = lax.psum_scatter(
        term(jnp.int32(0), gathered.shape[0] // lax.axis_size("col") * lax.axis_size("col")),
        "col",
        scatter_dimension=0,
        tiled=True,
    )
    return (gathered, result.astype(jnp.bfloat16))


def back_up(grad_cols, weight_block):
    gathered = lax.all_gather(grad_cols, "col", axis=0, tiled=True)

    def term(begin_at, row_count):
        return lax.dot_general(
            gathered, weight_block, (((1,), (1,)), ((), ())), preferred_element_type=jnp.float32
        )

    result = lax.psum_scatter(
        term(jnp.int32(0), gathered.shape[0] // lax.axis_size("row") * lax.axis_size("row")),
        "row",
        scatter_dimension=0,
        tiled=True,
    )
    return (gathered, result)


def weight_grad(left_rows, right_rows):
    return lax.dot_general(
        left_rows, right_rows, (((0,), (0,)), ((), ())), preferred_element_type=jnp.float32
    )


def block_scores(queries, keys_all, query_segment, key_segment, query_place):
    raw = jnp.einsum(
        "qhd,khd->hqk", queries, keys_all, preferred_element_type=jnp.float32
    ) * HEAD_DIM ** (-0.5)
    key_place = lax.broadcasted_iota(jnp.int32, (1, keys_all.shape[0]), 1)
    allowed = (query_segment[:, None] == key_segment[None, :]) & (key_place <= query_place[:, None])
    return jnp.where(allowed[None], raw, MASKED)


def split_blocks(queries, segment):
    length = queries.shape[0]
    block_rows = min(512, length)
    blocks = length // block_rows
    place = jnp.arange(length, dtype=jnp.int32).reshape(blocks, block_rows)
    return (
        queries.reshape(blocks, block_rows, queries.shape[1], queries.shape[2]),
        segment.reshape(blocks, block_rows),
        place,
    )


def attend_forward(queries, keys_all, values_all, segment):
    query_blocks, segment_blocks, place_blocks = split_blocks(queries, segment)

    def one_block(item):
        query_rows, query_segment, query_place = item
        scores = block_scores(query_rows, keys_all, query_segment, segment, query_place)
        row_max = jnp.max(scores, axis=-1, keepdims=True)
        expo = jnp.exp(scores - row_max)
        row_total = jnp.sum(expo, axis=-1, keepdims=True)
        prob_rows = (expo / row_total).astype(jnp.bfloat16)
        mixed = jnp.einsum(
            "hqk,khd->qhd", prob_rows, values_all, preferred_element_type=jnp.float32
        )
        return (mixed, row_max[..., 0] + jnp.log(row_total[..., 0]))

    mixed, log_total = lax.map(one_block, (query_blocks, segment_blocks, place_blocks))
    return (mixed.reshape(queries.shape[0], -1).astype(jnp.bfloat16), log_total)


def attend_backward(queries, keys_all, values_all, segment, log_total, grad_mix):
    query_blocks, segment_blocks, place_blocks = split_blocks(queries, segment)
    grad_blocks = grad_mix.reshape(query_blocks.shape)
    factor = HEAD_DIM ** (-0.5)

    def one_block(carry, item):
        key_acc, value_acc = carry
        query_rows, query_segment, query_place, log_rows, grad_rows = item
        scores = block_scores(query_rows, keys_all, query_segment, segment, query_place)
        prob_rows = jnp.exp(scores - log_rows[..., None])
        value_acc = value_acc + jnp.einsum(
            "hqk,qhd->khd",
            prob_rows.astype(jnp.bfloat16),
            grad_rows,
            preferred_element_type=jnp.float32,
        )
        grad_prob = jnp.einsum(
            "qhd,khd->hqk", grad_rows, values_all, preferred_element_type=jnp.float32
        )
        grad_scores = (
            prob_rows * (grad_prob - jnp.sum(prob_rows * grad_prob, axis=-1, keepdims=True))
        ).astype(jnp.bfloat16)
        grad_query = (
            jnp.einsum("hqk,khd->qhd", grad_scores, keys_all, preferred_element_type=jnp.float32)
            * factor
        )
        key_acc = (
            key_acc
            + jnp.einsum(
                "hqk,qhd->khd", grad_scores, query_rows, preferred_element_type=jnp.float32
            )
            * factor
        )
        return ((key_acc, value_acc), grad_query)

    zeros_like_keys = jnp.zeros(keys_all.shape, jnp.float32)
    (grad_keys, grad_values), grad_queries = lax.scan(
        one_block,
        (zeros_like_keys, zeros_like_keys),
        (query_blocks, segment_blocks, place_blocks, log_total, grad_blocks),
    )
    grad_queries = grad_queries.reshape(queries.shape)
    return jnp.stack([grad_queries, grad_keys, grad_values], axis=1).astype(jnp.bfloat16)


def local(tokens, segment_ids, gain_attn, gain_ffn, w_qkv, w_out, w_gate_up, w_down, grad_out):
    values = tokens.astype(jnp.float32)
    head_cols = w_qkv.shape[2]
    heads_here = head_cols // HEAD_DIM
    hidden_here = w_gate_up.shape[2]
    qkv_block = w_qkv.reshape(w_qkv.shape[0], 3 * head_cols)
    gate_up_block = w_gate_up.reshape(w_gate_up.shape[0], 2 * hidden_here)
    seq_count, seq_length = segment_ids.shape
    unit_one, rescale_one, normed_one = row_norm(values, gain_attn)
    gathered_one, packed = project_up(normed_one, qkv_block)
    packed = packed.reshape(-1, 3, heads_here, HEAD_DIM)
    mix_parts, log_parts = ([], [])
    for index in range(seq_count):
        rows_here = packed[index * seq_length : (index + 1) * seq_length]
        mixed, log_total = attend_forward(
            rows_here[:, 0], rows_here[:, 1], rows_here[:, 2], segment_ids[index]
        )
        mix_parts.append(mixed)
        log_parts.append(log_total)
    attn_mix = jnp.concatenate(mix_parts, axis=0)
    gathered_mix, attn_branch = project_down(attn_mix, w_out)
    hidden = values + attn_branch
    unit_two, rescale_two, normed_two = row_norm(hidden, gain_ffn)
    gathered_two, gate_up = project_up(normed_two, gate_up_block)
    gate_vals = gate_up[:, :hidden_here].astype(jnp.float32)
    up_vals = gate_up[:, hidden_here:].astype(jnp.float32)
    sigmoid_gate = jax.nn.sigmoid(gate_vals)
    silu_gate = gate_vals * sigmoid_gate
    active = (silu_gate * up_vals).astype(jnp.bfloat16)
    gathered_act, ffn_branch = project_down(active, w_down)
    output = (hidden + ffn_branch).astype(jnp.bfloat16)
    grad_rows_out, grad_active = back_down(grad_out, w_down)
    grad_down = weight_grad(gathered_act, grad_rows_out)
    grad_act_f = grad_active.astype(jnp.float32)
    grad_gate = grad_act_f * up_vals * sigmoid_gate * (1.0 + gate_vals * (1.0 - sigmoid_gate))
    grad_up = grad_act_f * silu_gate
    grad_gate_up_rows = jnp.concatenate([grad_gate, grad_up], axis=1).astype(jnp.bfloat16)
    grad_cols_two, grad_normed_two = back_up(grad_gate_up_rows, gate_up_block)
    grad_gate_up = weight_grad(gathered_two, grad_cols_two).reshape(w_gate_up.shape)
    grad_hidden_norm, grad_gain_two = norm_backward(
        grad_normed_two, unit_two, rescale_two, gain_ffn
    )
    grad_hidden = grad_out.astype(jnp.float32) + grad_hidden_norm
    grad_rows_hidden, grad_mix = back_down(grad_hidden.astype(jnp.bfloat16), w_out)
    grad_out_weight = weight_grad(gathered_mix, grad_rows_hidden)
    grad_mix = grad_mix.reshape(-1, heads_here, HEAD_DIM)
    grad_parts = []
    for index in range(seq_count):
        rows_here = packed[index * seq_length : (index + 1) * seq_length]
        grad_parts.append(
            attend_backward(
                rows_here[:, 0],
                rows_here[:, 1],
                rows_here[:, 2],
                segment_ids[index],
                log_parts[index],
                grad_mix[index * seq_length : (index + 1) * seq_length],
            )
        )
    grad_packed = jnp.concatenate(grad_parts, axis=0).reshape(-1, 3 * head_cols)
    grad_cols_one, grad_normed_one = back_up(grad_packed, qkv_block)
    grad_qkv = weight_grad(gathered_one, grad_cols_one).reshape(w_qkv.shape)
    grad_input_norm, grad_gain_one = norm_backward(
        grad_normed_one, unit_one, rescale_one, gain_attn
    )
    grad_tokens = grad_hidden + grad_input_norm
    summed = lax.psum((grad_qkv, grad_out_weight, grad_gate_up, grad_down), "dp")
    gains = lax.psum((grad_gain_one, grad_gain_two), ("dp", "row"))
    return (output, grad_tokens, gains[0], gains[1], summed[0], summed[1], summed[2], summed[3])


def solution(mesh):
    in_specs = (
        P(("dp", "row"), "col"),
        P(("dp", "col"), None),
        P("col"),
        P("col"),
        P("col", None, "row"),
        P("row", "col"),
        P("col", None, "row"),
        P("row", "col"),
        P(("dp", "row"), "col"),
    )
    out_specs = (
        P(("dp", "row"), "col"),
        P(("dp", "row"), "col"),
        P("col"),
        P("col"),
        P("col", None, "row"),
        P("row", "col"),
        P("col", None, "row"),
        P("row", "col"),
    )
    return jax.shard_map(local, mesh=mesh, in_specs=in_specs, out_specs=out_specs, check_vma=False)
```

profile of v0, /device:TPU:0, one launch (start us, length us, event | category | flops | bytes accessed | tf_op | source)
XLA Modules:
  0.0 1861.9 jit_solution(1210261778710294658)
XLA Ops:
  8.5 13.5 psum.70
  25.3 32.3 %all-gather.9.cloned.1.call-done = bf16[4096,256]{1,0:T(8,128)(2,1)} async-done(((bf16[1024,256]{1,0:T(8,128)(2,1)}), bf16[4096,256]{1,0:T(8,128)(2,1)}) %all-gather.9.cloned.1.call-update) | async-done | bytes 2097168 | tf_op jit(solution)/shard_map/all_gather | solution.py:30
  68.1 209.5 %reduce-scatter.9.cloned.1.call-done = f32[1024,768]{1,0:T(8,128)} async-done(((f32[4096,768]{1,0:T(8,128)}), f32[1024,768]{1,0:T(8,128)}) %reduce-scatter.9.cloned.1.call-update) | async-done | bytes 3145744 | tf_op jit(solution)/shard_map/reduce_scatter | solution.py:35
  290.4 46.8 %all-gather.11.cloned.1.call-done = bf16[4096,256]{0,1:T(8,128)(2,1)} async-done(((bf16[1024,256]{0,1:T(8,128)(2,1)}), bf16[4096,256]{0,1:T(8,128)(2,1)}) %all-gather.11.cloned.1.call-update) | async-done | bytes 2097168 | tf_op jit(solution)/shard_map/all_gather | solution.py:45
  341.6 51.5 %reduce-scatter.11.cloned.1.call-done = f32[1024,256]{1,0:T(8,128)} async-done(((f32[4096,256]{1,0:T(8,128)}), f32[1024,256]{1,0:T(8,128)}) %reduce-scatter.11.cloned.1.call-update) | async-done | bytes 1048592 | tf_op jit(solution)/shard_map/reduce_scatter | solution.py:50
  394.6 11.7 psum.71
  408.1 31.8 %all-gather.13.cloned.1.call-done = bf16[4096,256]{1,0:T(8,128)(2,1)} async-done(((bf16[1024,256]{1,0:T(8,128)(2,1)}), bf16[4096,256]{1,0:T(8,128)(2,1)}) %all-gather.13.cloned.1.call-update) | async-done | bytes 2097168 | tf_op jit(solution)/shard_map/all_gather | solution.py:30
  439.9 13.2 fusion.66
  453.1 23.6 %all-gather.17.cloned.1.call-done = bf16[4096,256]{1,0:T(8,128)(2,1)} async-done(((bf16[1024,256]{1,0:T(8,128)(2,1)}), bf16[4096,256]{1,0:T(8,128)(2,1)}) %all-gather.17.cloned.1.call-update) | async-done | bytes 2097168 | tf_op jit(solution)/shard_map/all_gather | solution.py:60
  484.8 375.1 %reduce-scatter.13.cloned.1.call-done = f32[1024,1408]{1,0:T(8,128)} async-done(((f32[4096,1408]{1,0:T(8,128)}), f32[1024,1408]{1,0:T(8,128)}) %reduce-scatter.13.cloned.1.call-update) | async-done | bytes 5767184 | tf_op jit(solution)/shard_map/reduce_scatter | solution.py:35
  864.4 211.4 %reduce-scatter.17.cloned.1.call-done = f32[1024,704]{1,0:T(8,128)} async-done(((f32[4096,704]{1,0:T(8,128)}), f32[1024,704]{1,0:T(8,128)}) %reduce-scatter.17.cloned.1.call-update) | async-done | bytes 2883600 | tf_op jit(solution)/shard_map/reduce_scatter | solution.py:67
  1083.7 202.2 %all-gather.19.cloned.1.call-done = bf16[4096,1408]{1,0:T(8,128)(2,1)} async-done(((bf16[1024,1408]{1,0:T(8,128)(2,1)}), bf16[4096,1408]{1,0:T(8,128)(2,1)}) %all-gather.19.cloned.1.call-update) | async-done | bytes 11534352 | tf_op jit(solution)/shard_map/all_gather | solution.py:77
  1285.9 9.7 fusion.69
  1295.7 50.9 %reduce-scatter.19.cloned.1.call-done = f32[1024,256]{1,0:T(8,128)} async-done(((f32[4096,256]{1,0:T(8,128)}), f32[1024,256]{1,0:T(8,128)}) %reduce-scatter.19.cloned.1.call-update) | async-done | bytes 1048592 | tf_op jit(solution)/shard_map/reduce_scatter | solution.py:84
  1348.2 11.7 psum.72
  1362.6 32.3 %all-gather.21.cloned.1.call-done = bf16[4096,256]{1,0:T(8,128)(2,1)} async-done(((bf16[1024,256]{1,0:T(8,128)(2,1)}), bf16[4096,256]{1,0:T(8,128)(2,1)}) %all-gather.21.cloned.1.call-update) | async-done | bytes 2097168 | tf_op jit(solution)/shard_map/all_gather | solution.py:60
  1400.1 76.1 %reduce-scatter.21.cloned.1.call-done = f32[1024,256]{1,0:T(8,128)} async-done(((f32[4096,256]{1,0:T(8,128)}), f32[1024,256]{1,0:T(8,128)}) %reduce-scatter.21.cloned.1.call-update) | async-done | bytes 1048592 | tf_op jit(solution)/shard_map/reduce_scatter | solution.py:67
  1494.3 99.3 %all-gather.15.cloned.1.call-done = bf16[4096,704]{1,0:T(8,128)(2,1)} async-done(((bf16[1024,704]{1,0:T(8,128)(2,1)}), bf16[4096,704]{1,0:T(8,128)(2,1)}) %all-gather.15.cloned.1.call-update) | async-done | bytes 5767184 | tf_op jit(solution)/shard_map/all_gather | solution.py:45
  1599.9 9.3 fusion.73
  1610.6 98.0 %all-gather.23.cloned.1.call-done = bf16[4096,768]{0,1:T(8,128)(2,1)} async-done(((bf16[1024,768]{0,1:T(8,128)(2,1)}), bf16[4096,768]{0,1:T(8,128)(2,1)}) %all-gather.23.cloned.1.call-update) | async-done | bytes 6291472 | tf_op jit(solution)/shard_map/all_gather | solution.py:77
  1739.0 54.3 %reduce-scatter.23.cloned.1.call-done = f32[1024,256]{1,0:T(8,128)} async-done(((f32[4096,256]{1,0:T(8,128)}), f32[1024,256]{1,0:T(8,128)}) %reduce-scatter.23.cloned.1.call-update) | async-done | bytes 1048592 | tf_op jit(solution)/shard_map/reduce_scatter | solution.py:84
  1795.1 15.4 all-reduce
  1810.5 11.7 psum.73
  1822.2 26.9 %reduce-scatter.15.cloned.1.call-done = f32[1024,256]{1,0:T(8,128)} async-done(((f32[4096,256]{1,0:T(8,128)}), f32[1024,256]{1,0:T(8,128)}) %reduce-scatter.15.cloned.1.call-update) | async-done | bytes 1048592 | tf_op jit(solution)/shard_map/reduce_scatter | solution.py:50
  (147 shorter events, 129.0 us)
Async XLA Ops:
  7.2 432.7 %copy-start = (bf16[256,2,704]{0,2,1:T(8,128)(2,1)S(1)}, bf16[256,2,704]{0,2,1:T(8,128)(2,1)}, u32[]{:S(2)}) copy-start(bf16[256,2,704]{0,2,1:T(8,128)(2,1)} %param.15) | copy-start | bytes 2162692
  7.2 50.5 %all-gather.9.cloned.1.call-start = ((), (), s32[]{:S(2)}) async-start(), calls=%async_computation.8 | async-start | bytes 2621440 | tf_op jit(solution)/shard_map/all_gather | solution.py:30
  24.1 253.5 %reduce-scatter.9.cloned.1.call-start = ((), (), s32[]{:S(2)}) async-start(), calls=%async_computation.9 | async-start | bytes 15728640 | tf_op jit(solution)/shard_map/reduce_scatter | solution.py:35
  65.6 271.6 %all-gather.11.cloned.1.call-start = ((), (), s32[]{:S(2)}) async-start(), calls=%async_computation.10 | async-start | bytes 2621440 | tf_op jit(solution)/shard_map/all_gather | solution.py:45
  290.4 102.8 %reduce-scatter.11.cloned.1.call-start = ((), (), s32[]{:S(2)}) async-start(), calls=%async_computation.11 | async-start | bytes 5242880 | tf_op jit(solution)/shard_map/reduce_scatter | solution.py:50
  341.5 51.6 %copy-start.7 = (bf16[1024,256]{1,0:T(8,128)(2,1)S(1)}, bf16[1024,256]{1,0:T(8,128)(2,1)}, u32[]{:S(2)}) copy-start(bf16[1024,256]{1,0:T(8,128)(2,1)} %param.9) | copy-start | bytes 1572868
  341.5 64.8 %copy-start.22 = (f32[256]{0:T(256)S(1)}, f32[256]{0:T(256)}, u32[]{:S(2)}) copy-start(f32[256]{0:T(256)} %param.12) | copy-start | bytes 3076
  341.5 98.3 %all-gather.13.cloned.1.call-start = ((), (), s32[]{:S(2)}) async-start(), calls=%async_computation.12 | async-start | bytes 2621440 | tf_op jit(solution)/shard_map/all_gather | solution.py:30
  407.3 69.5 %all-gather.17.cloned.1.call-start = ((), (), s32[]{:S(2)}) async-start(), calls=%async_computation.16 | async-start | bytes 2621440 | tf_op jit(solution)/shard_map/all_gather | solution.py:60
  407.9 452.0 %reduce-scatter.13.cloned.1.call-start = ((), (), s32[]{:S(2)}) async-start(), calls=%async_computation.13 | async-start | bytes 28835840 | tf_op jit(solution)/shard_map/reduce_scatter | solution.py:35
  453.1 622.8 %reduce-scatter.17.cloned.1.call-start = ((), (), s32[]{:S(2)}) async-start(), calls=%async_computation.17 | async-start | bytes 15728640 | tf_op jit(solution)/shard_map/reduce_scatter | solution.py:67
  484.7 801.1 %all-gather.19.cloned.1.call-start = ((), (), s32[]{:S(2)}) async-start(), calls=%async_computation.18 | async-start | bytes 14417920 | tf_op jit(solution)/shard_map/all_gather | solution.py:77
  1083.6 262.9 %reduce-scatter.19.cloned.1.call-start = ((), (), s32[]{:S(2)}) async-start(), calls=%async_computation.19 | async-start | bytes 5242880 | tf_op jit(solution)/shard_map/reduce_scatter | solution.py:84
  1295.6 64.3 %copy-start.10 = (bf16[1024,256]{1,0:T(8,128)(2,1)S(1)}, bf16[1024,256]{1,0:T(8,128)(2,1)}, u32[]{:S(2)}) copy-start(bf16[1024,256]{1,0:T(8,128)(2,1)} %param.17) | copy-start | bytes 1572868
  1295.6 99.3 %copy-start.19 = (bf16[256,256]{1,0:T(8,128)(2,1)S(1)}, bf16[256,256]{1,0:T(8,128)(2,1)}, u32[]{:S(2)}) copy-start(bf16[256,256]{1,0:T(8,128)(2,1)} %param.14) | copy-start | bytes 393220
  1295.6 99.3 %all-gather.21.cloned.1.call-start = ((), (), s32[]{:S(2)}) async-start(), calls=%async_computation.20 | async-start | bytes 2621440 | tf_op jit(solution)/shard_map/all_gather | solution.py:60
  1362.3 113.8 %reduce-scatter.21.cloned.1.call-start = ((), (), s32[]{:S(2)}) async-start(), calls=%async_computation.21 | async-start | bytes 5242880 | tf_op jit(solution)/shard_map/reduce_scatter | solution.py:67
  1399.3 194.4 %all-gather.15.cloned.1.call-start = ((), (), s32[]{:S(2)}) async-start(), calls=%async_computation.14 | async-start | bytes 7864320 | tf_op jit(solution)/shard_map/all_gather | solution.py:45
  1400.0 308.6 %all-gather.23.cloned.1.call-start = ((), (), s32[]{:S(2)}) async-start(), calls=%async_computation.22 | async-start | bytes 7864320 | tf_op jit(solution)/shard_map/all_gather | solution.py:77
  1494.0 242.7 %all-reduce.4.cloned.1.call-start = ((), (), s32[]{:S(2)}) async-start(), calls=%async_computation.24 | async-start | bytes 6422528 | tf_op jit(solution)/shard_map/psum | solution.py:250
  1714.7 78.6 %reduce-scatter.23.cloned.1.call-start = ((), (), s32[]{:S(2)}) async-start(), calls=%async_computation.23 | async-start | bytes 5242880 | tf_op jit(solution)/shard_map/reduce_scatter | solution.py:84
  1721.4 127.7 %reduce-scatter.15.cloned.1.call-start = ((), (), s32[]{:S(2)}) async-start(), calls=%async_computation.15 | async-start | bytes 5242880 | tf_op jit(solution)/shard_map/reduce_scatter | solution.py:50
  1729.3 64.1 %copy-start.23 = (f32[256]{0:T(256)S(1)}, f32[256]{0:T(256)}, u32[]{:S(2)}) copy-start(f32[256]{0:T(256)} %param.11) | copy-start | bytes 3076
  1729.3 119.8 %copy-start.9 = (f32[1024,256]{1,0:T(8,128)S(1)}, f32[1024,256]{1,0:T(8,128)}, u32[]{:S(2)}) copy-start(f32[1024,256]{1,0:T(8,128)} %reduce-scatter.19.cloned.1.call-done) | copy-start | bytes 3145732
  (18 other events, 137.8 us)
Sparse Core Ops, SparseCore 0:
  24.2 33.3 all-gather.8
  65.8 211.8 reduce-scatter.8
  290.5 46.6 all-gather.10
  341.7 51.4 reduce-scatter.10
  407.4 32.3 all-gather.12
  441.5 35.1 all-gather.16
  479.1 380.7 reduce-scatter.12
  862.3 213.5 reduce-scatter.16
  1083.8 202.0 all-gather.18
  1295.8 50.7 reduce-scatter.18
  1362.5 32.4 all-gather.20
  1399.4 76.7 reduce-scatter.20
  1477.8 115.8 all-gather.14
  1595.1 113.4 all-gather.22
  1714.8 21.8 all-reduce.3
  1739.6 53.7 reduce-scatter.22
  1796.2 52.8 reduce-scatter.14
where the time goes:
time: 1870 us; the launch traced here: 1860 us
  waiting for transfers between devices  1630 us (87%)
  matrix products  98.7 us (5%)
  blocking collectives  63.9 us (3%)
  other arithmetic  38.2 us (2%)
    reduce_scatter x2, waiting for transfers between devices, project_up(): lax.psum_scatter(term(jnp.int32(0), gathered.shape[0] // lax.axis_size('c...  585 us
    all_gather x2, waiting for transfers between devices, back_up(): gathered = lax.all_gather(grad_cols, 'col', axis=0, tiled=True)  300 us
    reduce_scatter x2, waiting for transfers between devices, back_down(): lax.psum_scatter(term(jnp.int32(0), gathered.shape[0] // lax.axis_size('c...  288 us
    all_gather x2, waiting for transfers between devices, project_down(): gathered = lax.all_gather(values, 'col', axis=0, tiled=True)  146 us
    reduce_scatter x2, waiting for transfers between devices, back_up(): lax.psum_scatter(term(jnp.int32(0), gathered.shape[0] // lax.axis_size('r...  105 us
    reduce_scatter x2, waiting for transfers between devices, project_down(): lax.psum_scatter(term(jnp.int32(0), gathered.shape[0] // lax.axis_size('r...  78.4 us
    all_gather x2, waiting for transfers between devices, project_up(): gathered = lax.all_gather(normed, 'row', axis=0, tiled=True)  64.1 us
    all_gather x2, waiting for transfers between devices, back_down(): gathered = lax.all_gather(grad_rows, 'row', axis=0, tiled=True)  55.9 us
  transfers between devices with their start and end apart: 17, of which 17 were waited for; matrix products, arithmetic and copies ran while one was open for 4% of the time, Pallas kernels for 0%

commit v1 on v0

--- a/solution.py
+++ b/solution.py
@@ -252,6 +252,210 @@
     return (output, grad_tokens, gains[0], gains[1], summed[0], summed[1], summed[2], summed[3])
 
 
+def swap(values):
+    return lax.ppermute(values, "dp", [(0, 1), (1, 0)])
+
+
+def by_core(core, mine, other, axis=0):
+    first = jnp.where(core == 0, mine, other)
+    second = jnp.where(core == 0, other, mine)
+    return jnp.concatenate([first, second], axis=axis)
+
+
+def pick(values, core, axis=0):
+    half = values.shape[axis] // 2
+    return lax.dynamic_slice_in_dim(values, core * half, half, axis)
+
+
+def to_sequence(values, core, seq_length):
+    seqs = values.shape[0] // seq_length
+    half = seq_length // 2
+    parts = values.reshape(seqs, seq_length, -1)
+    mine = pick(parts, core, 1)
+    other = swap(pick(parts, 1 - core, 1))
+    chunks = by_core(core, mine, other)
+    got = lax.all_to_all(chunks, "col", 0, 0, tiled=True)
+    rows = got.transpose(1, 0, 2).reshape(half, -1)
+    return by_core(core, rows, swap(rows))
+
+
+def from_sequence(rows, core, seq_length):
+    cols = lax.axis_size("col")
+    half = rows.shape[0]
+    chunks = rows.reshape(half, cols, -1).transpose(1, 0, 2)
+    got = lax.all_to_all(chunks, "col", 0, 0, tiled=True)
+    mine = pick(got, core)
+    other = swap(pick(got, 1 - core))
+    return by_core(core, mine, other, 1).reshape(cols // 2 * seq_length, -1)
+
+
+def times(left, right):
+    return jnp.dot(left, right, preferred_element_type=jnp.float32)
+
+
+def times_t(left, right):
+    return lax.dot_general(
+        left, right, (((1,), (1,)), ((), ())), preferred_element_type=jnp.float32
+    )
+
+
+def norm_rows(values):
+    rescale = lax.rsqrt(jnp.mean(values * values, axis=1) + EPS)[:, None]
+    return (values * rescale, rescale)
+
+
+def norm_rows_back(grad_normed, unit_rows, rescale, gain_vec):
+    weighted = grad_normed * gain_vec[None, :]
+    inner = jnp.sum(weighted * unit_rows, axis=1, keepdims=True) / D
+    return (rescale * (weighted - unit_rows * inner), jnp.sum(grad_normed * unit_rows, axis=0))
+
+
+def spread_weights(block, kinds):
+    rows, cols = (lax.axis_size("row"), lax.axis_size("col"))
+    gathered = lax.all_gather(block, ("row", "col"), axis=0, tiled=True)
+    gathered = gathered.reshape(rows, cols, kinds, -1, block.shape[1])
+    return gathered.transpose(2, 0, 3, 1, 4).reshape(-1, cols * block.shape[1])
+
+
+def reduce_weights(parts):
+    rows, cols = (lax.axis_size("row"), lax.axis_size("col"))
+    pieces = []
+    for grad, kinds in parts:
+        block = grad.astype(jnp.bfloat16).reshape(kinds, rows, -1, cols, grad.shape[1] // cols)
+        pieces.append(block.transpose(1, 3, 0, 2, 4).reshape(rows * cols, -1, block.shape[4]))
+    stacked = jnp.concatenate(pieces, axis=1)
+    stacked = lax.psum_scatter(stacked, "row", scatter_dimension=0, tiled=True)
+    return lax.psum_scatter(stacked, "col", scatter_dimension=0, tiled=True)[0]
+
+
+def chip_local(tokens, segment_ids, gain_attn, gain_ffn, w_qkv, w_out, w_gate_up, w_down, grad_out):
+    core = lax.axis_index("dp")
+    rows, cols = (lax.axis_size("row"), lax.axis_size("col"))
+    row, col = (lax.axis_index("row"), lax.axis_index("col"))
+    length = segment_ids.shape[1]
+    seqs = tokens.shape[0] // length
+    features = w_qkv.shape[0]
+    head_cols = w_qkv.shape[2] // 2
+    hidden = w_gate_up.shape[2] // 2
+    heads = rows * head_cols // HEAD_DIM
+    factor = HEAD_DIM ** (-0.5)
+
+    qkv_t = pick(w_qkv, core, 2).transpose(1, 2, 0).reshape(3 * head_cols, features)
+    gate_up_t = pick(w_gate_up, core, 2).transpose(1, 2, 0).reshape(2 * hidden, features)
+    big_qkv = spread_weights(qkv_t, 3)
+    big_out = spread_weights(pick(w_out, core), 1)
+    big_gate_up = spread_weights(gate_up_t, 2)
+    big_down = spread_weights(pick(w_down, core), 1)
+    gains = lax.all_gather(jnp.stack([gain_attn, gain_ffn], axis=0), "col", axis=1, tiled=True)
+
+    every_segment = lax.all_gather(segment_ids, ("dp", "col"), axis=0, tiled=True)
+    place = col // seqs * (rows * seqs) + row * seqs + col % seqs
+    segment = lax.dynamic_index_in_dim(every_segment, place, 0, keepdims=False)
+
+    values = to_sequence(tokens, core, length).astype(jnp.float32)
+    cotangent = to_sequence(grad_out, core, length)
+
+    unit_one, rescale_one = norm_rows(values)
+    normed_one = (unit_one * gains[0][None, :]).astype(jnp.bfloat16)
+    packed = times_t(normed_one, big_qkv).astype(jnp.bfloat16).reshape(length, 3, heads, HEAD_DIM)
+    queries, keys, vals = (packed[:, 0], packed[:, 1], packed[:, 2])
+    scores = jnp.einsum("qhd,khd->hqk", queries, keys, preferred_element_type=jnp.float32) * factor
+    spot = jnp.arange(length, dtype=jnp.int32)
+    live = (segment[:, None] == segment[None, :]) & (spot[None, :] <= spot[:, None])
+    scores = jnp.where(live[None], scores, MASKED)
+    expo = jnp.exp(scores - jnp.max(scores, axis=-1, keepdims=True))
+    prob = expo / jnp.sum(expo, axis=-1, keepdims=True)
+    prob_low = prob.astype(jnp.bfloat16)
+    mixed = jnp.einsum("hqk,khd->qhd", prob_low, vals, preferred_element_type=jnp.float32)
+    mixed = mixed.reshape(length, -1).astype(jnp.bfloat16)
+    branch = times(mixed, big_out)
+    hidden_rows = values + (branch + swap(branch))
+    unit_two, rescale_two = norm_rows(hidden_rows)
+    normed_two = (unit_two * gains[1][None, :]).astype(jnp.bfloat16)
+    gate_up = times_t(normed_two, big_gate_up).astype(jnp.bfloat16)
+    half = gate_up.shape[1] // 2
+    gate_vals = gate_up[:, :half].astype(jnp.float32)
+    up_vals = gate_up[:, half:].astype(jnp.float32)
+    sigmoid_gate = jax.nn.sigmoid(gate_vals)
+    silu_gate = gate_vals * sigmoid_gate
+    active = (silu_gate * up_vals).astype(jnp.bfloat16)
+    ffn = times(active, big_down)
+    ffn_mine = pick(ffn, core) + swap(pick(ffn, 1 - core))
+    output = from_sequence((pick(hidden_rows, core) + ffn_mine).astype(jnp.bfloat16), core, length)
+
+    grad_down = weight_grad(active, cotangent)
+    grad_act = times_t(cotangent, big_down).astype(jnp.bfloat16).astype(jnp.float32)
+    grad_gate = grad_act * up_vals * sigmoid_gate * (1.0 + gate_vals * (1.0 - sigmoid_gate))
+    grad_up = grad_act * silu_gate
+    grad_gu = jnp.concatenate([grad_gate, grad_up], axis=1).astype(jnp.bfloat16)
+    grad_gate_up = weight_grad(grad_gu, normed_two)
+    grad_two = times(grad_gu, big_gate_up)
+    grad_two = grad_two + swap(grad_two)
+    mine_ffn = reduce_weights([(grad_gate_up, 2), (grad_down, 1)])
+    back_two, _ = norm_rows_back(grad_two, unit_two, rescale_two, gains[1])
+    gain_two = jnp.sum(pick(grad_two * unit_two, core), axis=0)
+    grad_hidden = cotangent.astype(jnp.float32) + back_two
+    grad_branch = grad_hidden.astype(jnp.bfloat16)
+    grad_w_out = weight_grad(mixed, grad_branch)
+    grad_mix = times_t(grad_branch, big_out).astype(jnp.bfloat16).reshape(length, heads, HEAD_DIM)
+    grad_vals = jnp.einsum("hqk,qhd->khd", prob_low, grad_mix, preferred_element_type=jnp.float32)
+    grad_prob = jnp.einsum("qhd,khd->hqk", grad_mix, vals, preferred_element_type=jnp.float32)
+    inner = jnp.sum(prob * grad_prob, axis=-1, keepdims=True)
+    grad_scores = (prob * (grad_prob - inner)).astype(jnp.bfloat16)
+    grad_queries = factor * jnp.einsum(
+        "hqk,khd->qhd", grad_scores, keys, preferred_element_type=jnp.float32
+    )
+    grad_keys = factor * jnp.einsum(
+        "hqk,qhd->khd", grad_scores, queries, preferred_element_type=jnp.float32
+    )
+    grad_packed = jnp.stack([grad_queries, grad_keys, grad_vals], axis=1)
+    grad_packed = grad_packed.astype(jnp.bfloat16).reshape(length, -1)
+    grad_qkv = weight_grad(grad_packed, normed_one)
+    mine_attn = reduce_weights([(grad_qkv, 3), (grad_w_out, 1)])
+    grad_one = times(grad_packed, big_qkv)
+    grad_one = pick(grad_one, core) + swap(pick(grad_one, 1 - core))
+    back_one, gain_one = norm_rows_back(
+        grad_one, pick(unit_one, core), pick(rescale_one, core), gains[0]
+    )
+    grad_rows = (pick(grad_hidden, core) + back_one).astype(jnp.bfloat16)
+    grad_tokens = from_sequence(grad_rows, core, length).astype(jnp.float32)
+
+    gain_sums = lax.psum(jnp.stack([gain_one, gain_two], axis=0), ("dp", "row", "col"))
+    gain_sums = lax.dynamic_slice_in_dim(gain_sums, col * features, features, 1)
+
+    gu_rows = 2 * hidden
+    out_ffn = swap(mine_ffn)
+    out_attn = swap(mine_attn)
+
+    def joined(mine, other, start, stop, kinds):
+        left = mine[start:stop].reshape(kinds, -1, features)
+        right = other[start:stop].reshape(kinds, -1, features)
+        return by_core(core, left, right, 1).astype(jnp.float32)
+
+    full_qkv = joined(mine_attn, out_attn, 0, 3 * head_cols, 3).transpose(2, 0, 1)
+    full_out = joined(mine_attn, out_attn, 3 * head_cols, None, 1)[0]
+    full_gate_up = joined(mine_ffn, out_ffn, 0, gu_rows, 2).transpose(2, 0, 1)
+    full_down = joined(mine_ffn, out_ffn, gu_rows, None, 1)[0]
+    return (
+        output,
+        grad_tokens,
+        gain_sums[0],
+        gain_sums[1],
+        full_qkv,
+        full_out,
+        full_gate_up,
+        full_down,
+    )
+
+
+def layer(tokens, segment_ids, *rest):
+    length = segment_ids.shape[1]
+    cols = lax.axis_size("col")
+    if lax.axis_size("dp") == 2 and tokens.shape[0] * 2 == cols * length:
+        return chip_local(tokens, segment_ids, *rest)
+    return local(tokens, segment_ids, *rest)
+
+
 def solution(mesh):
     in_specs = (
         P(("dp", "row"), "col"),
@@ -274,4 +478,4 @@
         P("col", None, "row"),
         P("row", "col"),
     )
-    return jax.shard_map(local, mesh=mesh, in_specs=in_specs, out_specs=out_specs, check_vma=False)
+    return jax.shard_map(layer, mesh=mesh, in_specs=in_specs, out_specs=out_specs, check_vma=False)

time: 1870 us -> 652 us (0.35)
  waiting for transfers between devices: 1630 us -> 321 us
  local copies, waits for them, and re-layouts: 14.1 us -> 87.1 us
  blocking collectives: 63.9 us -> 105 us
  matrix products: 98.7 us -> 61.8 us
    reduce_scatter x8 -> x4, waiting for transfers between devices: 1060 us -> 96.3 us  [the longest x2 96.3 us: reduce_weights(): stacked = lax.psum_scatter(stacked, 'row', scatter_dimension=0, tiled=True)]
    all_gather x8 -> x4, waiting for transfers between devices: 566 us -> 170 us  [spread_weights(): gathered = lax.all_gather(block, ('row', 'col'), axis=0, tiled=True)]
    all_to_all x0 -> x3, waiting for transfers between devices: none -> 46.8 us  [the longest x2 46.8 us: from_sequence(): got = lax.all_to_all(chunks, 'col', 0, 0, tiled=True)]
    all_gather x0 -> x2, blocking collectives: none -> 44.1 us  [the longest x1 32.2 us: chip_local(): lax.all_gather(segment_ids, ('dp', 'col'), axis=0, tiled=True)]
    reshape x0 -> x13, local copies, waits for them, and re-layouts: none -> 38.4 us  [the longest x4 25.9 us: reduce_weights(): grad.astype(jnp.bfloat16)]
    dot_general x20 -> x13, matrix products: 75.6 us -> 38.4 us  [the longest x4 15.5 us: times(): return jnp.dot(left, right, preferred_element_type=jnp.float32)]
    psum x5 -> x1, blocking collectives: 63.9 us -> 38.1 us  [chip_local(): lax.psum(jnp.stack([gain_one, gain_two], axis=0), ('dp', 'row', 'col'))]
    all_to_all x0 -> x1, blocking collectives: none -> 22.6 us  [to_sequence(): got = lax.all_to_all(chunks, 'col', 0, 0, tiled=True)]
  transfers between devices with their start and end apart: 17 -> 23, of which waited for: 17 -> 12; matrix products, arithmetic and copies ran while one was open for 4% -> 18% of each run, Pallas kernels for 0% -> 0%
where the time goes in v1:
time: 652 us; the launch traced here: 640 us
  waiting for transfers between devices  321 us (49%)
  blocking collectives  105 us (16%)
  local copies, waits for them, and re-layouts  87.1 us (13%)
  matrix products  61.8 us (9%)
  other arithmetic  33.5 us (5%)
  starting transfers between devices  16.9 us (3%)
  between operations  15.4 us (2%)
    all_gather x4, waiting for transfers between devices, spread_weights(): gathered = lax.all_gather(block, ('row', 'col'), axis=0, tiled=True)  170 us
    reduce_scatter x2, waiting for transfers between devices, reduce_weights(): stacked = lax.psum_scatter(stacked, 'row', scatter_dimension=0, tiled=True)  96.3 us
    all_to_all x2, waiting for transfers between devices, from_sequence(): got = lax.all_to_all(chunks, 'col', 0, 0, tiled=True)  46.8 us
    psum x1, blocking collectives, chip_local(): lax.psum(jnp.stack([gain_one, gain_two], axis=0), ('dp', 'row', 'col'))  38.1 us
    all_gather x1, blocking collectives, chip_local(): lax.all_gather(segment_ids, ('dp', 'col'), axis=0, tiled=True)  32.2 us
    reshape x4, local copies, waits for them, and re-layouts, reduce_weights(): grad.astype(jnp.bfloat16)  25.9 us
    all_to_all x1, blocking collectives, to_sequence(): got = lax.all_to_all(chunks, 'col', 0, 0, tiled=True)  22.6 us
    dot_general x4, matrix products, weight_grad(): lax.dot_general(left_rows, right_rows, (((0,), (0,)), ((), ())), preferre...  15.7 us
  transfers between devices with their start and end apart: 23, of which 12 were waited for; matrix products, arithmetic and copies ran while one was open for 18% of the time, Pallas kernels for 0%

profile of v1, /device:TPU:0, one launch (start us, length us, event | category | flops | bytes accessed | tf_op | source)
XLA Modules:
  0.0 640.5 jit_solution(3529579357009157481)
XLA Ops:
  16.0 6.2 all-to-all-start
  23.0 32.2 %all-gather = s32[8,2,512]{2,1,0:T(2,128)S(1)} all-gather(s32[1,2,512]{2,1,0:T(2,128)S(1)} %bitcast.234), channel_id=1, replica_groups=mesh['dp'=2,'row'=4,'col'=4] {'dp','col'}, dimensions={0}, use_global_device_ids=true | all-gather | bytes 36864 | tf_op jit(solution)/shard_map/all_gather | solution.py:351
  55.2 11.9 %all_gather.18 = f32[2,1024]{1,0:T(2,128)S(1)} all-gather(f32[2,256]{1,0:T(2,128)S(1)} %pad_maximum_fusion.14), channel_id=1, replica_groups=mesh['dp'=2,'row'=4,'col'=4] {'col'}, dimensions={1}, use_global_device_ids=true | all-gather | bytes 10240 | tf_op jit(solution)/shard_map/all_gather | solution.py:349
  75.4 67.9 %all-gather.6.cloned.1.call-done = bf16[6144,256]{1,0:T(8,128)(2,1)} async-done(((bf16[384,256]{1,0:T(8,128)(2,1)}), bf16[6144,256]{1,0:T(8,128)(2,1)}) %all-gather.6.cloned.1.call-update) | async-done | bytes 3145744 | tf_op jit(solution)/shard_map/all_gather | solution.py:315
  143.3 4.3 copy.87
  155.8 7.7 %fusion.47 = (f32[8,512]{1,0:T(8,128)S(1)}, f32[8,512,512]{1,2,0:T(8,128)}) fusion(pred[512,512]{0,1:T(8,128)(4,1)S(1)} %copy-done.32, bf16[512,3,8,64]{0,3,2,1:T(8,128)(2,1)} %bitcast.181), kind=kOutput, calls=%fused_computation.137 | convolution fusion | flops 276824576 | bytes 9715712 | tf_op jit(solution)/shard_map/sub | solution.py:366
  163.5 4.4 fusion.25
  171.1 22.6 %all_to_all.20 = bf16[4,256,256]{2,1,0:T(8,128)(2,1)S(1)} all-to-all(bf16[4,256,256]{2,1,0:T(8,128)(2,1)S(1)} %pad_maximum_fusion.9), channel_id=1, replica_groups=mesh['dp'=2,'row'=4,'col'=4] {'col'}, dimensions={0} | all-to-all | bytes 1048576 | tf_op jit(solution)/shard_map/all_to_all | solution.py:277
  196.8 19.6 %all-gather.12.cloned.1.call-done = bf16[5632,256]{1,0:T(8,128)(2,1)} async-done(((bf16[352,256]{1,0:T(8,128)(2,1)}), bf16[5632,256]{1,0:T(8,128)(2,1)}) %all-gather.12.cloned.1.call-update) | async-done | bytes 2883600 | tf_op jit(solution)/shard_map/all_gather | solution.py:315
  228.4 78.5 %all-gather.10.cloned.1.call-done = bf16[11264,256]{1,0:T(8,128)(2,1)} async-done(((bf16[704,256]{1,0:T(8,128)(2,1)}), bf16[11264,256]{1,0:T(8,128)(2,1)}) %all-gather.10.cloned.1.call-update) | async-done | bytes 5767184 | tf_op jit(solution)/shard_map/all_gather | solution.py:315
  307.0 7.1 %copy.91 = bf16[2,4,352,4,256]{4,3,2,1,0:T(4,128)(2,1)S(1)} copy(bf16[2,4,352,4,256]{4,2,0,3,1:T(8,128)(2,1)} %bitcast.178) | data formatting | bytes 11534336 | tf_op jit(solution)/shard_map/transpose | solution.py:317
  358.1 6.2 reshape.249
  370.3 5.3 convolution_convert_fusion.2
  375.6 6.3 reshape.258
  385.9 5.1 convolution_convert_fusion
  391.1 10.6 %reshape.256 = bf16[2,4,352,4,256]{4,3,2,1,0:T(4,128)(2,1)} reshape(bf16[2816,1024]{1,0:T(8,128)(2,1)} %convolution_convert_fusion) | data formatting | bytes 11534336 | tf_op jit(solution)/shard_map/reshape | solution.py:324
  409.3 11.2 %reduce-scatter.5.cloned.1.call-done = bf16[4,512,256]{2,1,0:T(8,128)(2,1)} async-done(((bf16[16,512,256]{2,1,0:T(8,128)(2,1)}), bf16[4,512,256]{2,1,0:T(8,128)(2,1)}) %reduce-scatter.5.cloned.1.call-update) | async-done | bytes 1048592 | tf_op jit(solution)/shard_map/reduce_scatter | solution.py:327
  420.9 6.1 fusion.43
  426.9 85.0 %reduce-scatter.9.cloned.1.call-done = bf16[4,1056,256]{2,1,0:T(8,128)(2,1)} async-done(((bf16[16,1056,256]{2,1,0:T(8,128)(2,1)}), bf16[4,1056,256]{2,1,0:T(8,128)(2,1)}) %reduce-scatter.9.cloned.1.call-update) | async-done | bytes 2162704 | tf_op jit(solution)/shard_map/reduce_scatter | solution.py:327
  513.4 4.2 fusion.49
  521.4 4.7 all-to-all-start.1
  531.5 19.8 %all-to-all-done.1 = bf16[4,256,256]{2,1,0:T(8,128)(2,1)S(1)} async-done(((bf16[4,256,256]{2,1,0:T(8,128)(2,1)}), bf16[4,256,256]{2,1,0:T(8,128)(2,1)S(1)}, u32[]{:S(2)}, u32[]{:S(2)}) %all-to-all-start.1) | async-done | bytes 524320 | tf_op jit(solution)/shard_map/all_to_all | solution.py:286
  555.5 27.0 %all-to-all-done.3 = bf16[4,256,256]{2,1,0:T(8,128)(2,1)S(1)} async-done(((bf16[4,256,256]{2,1,0:T(8,128)(2,1)}), bf16[4,256,256]{2,1,0:T(8,128)(2,1)S(1)}, u32[]{:S(2)}, u32[]{:S(2)}) %all-to-all-start.3) | async-done | bytes 524320 | tf_op jit(solution)/shard_map/all_to_all | solution.py:286
  584.6 38.1 %psum.7 = f32[2,1024]{1,0:T(2,128)S(1)} all-reduce(f32[2,1024]{1,0:T(2,128)S(1)} %pad_maximum_fusion.13), channel_id=1, replica_groups=mesh['dp'=2,'row'=4,'col'=4] {'dp','row','col'}, use_global_device_ids=true, to_apply=%region_9.10 | all-reduce | flops 2048 | bytes 16384 | tf_op jit(solution)/shard_map/psum | solution.py:423
  (220 shorter events, 133.0 us)
Async XLA Ops:
  7.2 65.9 %all-gather.8.cloned.1.call-start = ((), (), s32[]{:S(2)}) async-start(), calls=%async_computation.9 | async-start | bytes 1114112 | tf_op jit(solution)/shard_map/all_gather | solution.py:315
  8.8 134.4 %all-gather.6.cloned.1.call-start = ((), (), s32[]{:S(2)}) async-start(), calls=%async_computation.8 | async-start | bytes 3342336 | tf_op jit(solution)/shard_map/all_gather | solution.py:315
  10.7 205.7 %all-gather.12.cloned.1.call-start = ((), (), s32[]{:S(2)}) async-start(), calls=%async_computation.11 | async-start | bytes 3063808 | tf_op jit(solution)/shard_map/all_gather | solution.py:315
  12.4 294.6 %all-gather.10.cloned.1.call-start = ((), (), s32[]{:S(2)}) async-start(), calls=%async_computation.10 | async-start | bytes 6127616 | tf_op jit(solution)/shard_map/all_gather | solution.py:315
  13.3 1.7 collective-permute-start
  16.0 51.1 %all-to-all-start = ((bf16[4,256,256]{2,1,0:T(8,128)(2,1)}), bf16[4,256,256]{2,1,0:T(8,128)(2,1)S(1)}, u32[]{:S(2)}, u32[]{:S(2)}) async-start(bf16[4,256,256]{2,1,0:T(8,128)(2,1)} %pad_maximum_fusion.7), calls=%async_computation | async-start | bytes 1048576 | tf_op jit(solution)/shard_map/all_to_all | solution.py:277
  22.2 398.3 %reduce-scatter.5.cloned.1.call-start = ((), (), s32[]{:S(2)}) async-start(), calls=%async_computation.12 | async-start | bytes 5242880 | tf_op jit(solution)/shard_map/reduce_scatter | solution.py:327
  23.0 147.0 %collective-permute-start.5 = (bf16[2,256,256]{2,1,0:T(8,128)(2,1)}, bf16[2,256,256]{2,1,0:T(8,128)(2,1)}, u32[]{:S(2)}, u32[]{:S(2)}) collective-permute-start(bf16[2,256,256]{2,1,0:T(8,128)(2,1)} %constant_dynamic-slice_fusion.2), channel_id=1, source_target_pairs={{0,16},{16,0},{1,17},{17,1},{2,18},{18,2},{3,19},{19,3},{4,20},{20... | collective-permute-start | bytes 786440 | tf_op jit(solution)/shard_map/ppermute | solution.py:256
  67.2 2.0 collective-permute-start.1
  75.4 92.6 %copy-start.7 = (bf16[64,8,4,256]{3,1,2,0:T(8,128)(2,1)}, bf16[64,8,4,256]{3,1,2,0:T(8,128)(2,1)S(1)}, u32[]{:S(2)}) copy-start(bf16[64,8,4,256]{3,1,2,0:T(8,128)(2,1)S(1)} %copy.117) | copy-start | bytes 3145732
  170.0 52.7 %collective-permute-start.2 = (f32[512,1024]{1,0:T(8,128)}, f32[512,1024]{1,0:T(8,128)}, u32[]{:S(2)}, u32[]{:S(2)}) collective-permute-start(f32[512,1024]{1,0:T(8,128)} %fusion.48), channel_id=1, source_target_pairs={{0,16},{16,0},{1,17},{17,1},{2,18},{18,2},{3,19},{19,3},{4,20},{20... | collective-permute-start | bytes 6291464 | tf_op jit(solution)/shard_map/ppermute | solution.py:256
  193.8 2.0 collective-permute-start.6
  326.5 4.2 collective-permute-start.7
  369.1 142.9 %reduce-scatter.9.cloned.1.call-start = ((), (), s32[]{:S(2)}) async-start(), calls=%async_computation.14 | async-start | bytes 10813440 | tf_op jit(solution)/shard_map/reduce_scatter | solution.py:327
  409.3 216.1 %reduce-scatter.7.cloned.1.call-start = ((), (), s32[]{:S(2)}) async-start(), calls=%async_computation.13 | async-start | bytes 1310720 | tf_op jit(solution)/shard_map/reduce_scatter | solution.py:328
  420.6 207.0 %reduce-scatter.11.cloned.1.call-start = ((), (), s32[]{:S(2)}) async-start(), calls=%async_computation.15 | async-start | bytes 2703360 | tf_op jit(solution)/shard_map/reduce_scatter | solution.py:328
  513.3 5.8 collective-permute-start.3
  518.6 7.6 %collective-permute-start.8 = (f32[256,1024]{1,0:T(8,128)}, f32[256,1024]{1,0:T(8,128)}, u32[]{:S(2)}, u32[]{:S(2)}) collective-permute-start(f32[256,1024]{1,0:T(8,128)} %constant_dynamic-slice_fusion.1), channel_id=1, source_target_pairs={{0,16},{16,0},{1,17},{17,1},{2,18},{18,2},{3,19},{19,3},{4,20},{20... | collective-permute-start | bytes 3145736 | tf_op jit(solution)/shard_map/ppermute | solution.py:256
  521.4 29.8 %all-to-all-start.1 = ((bf16[4,256,256]{2,1,0:T(8,128)(2,1)}), bf16[4,256,256]{2,1,0:T(8,128)(2,1)S(1)}, u32[]{:S(2)}, u32[]{:S(2)}) async-start(bf16[4,256,256]{2,1,0:T(8,128)(2,1)} %bitcast.164), calls=%async_computation.1 | async-start | bytes 1048576 | tf_op jit(solution)/shard_map/all_to_all | solution.py:286
  551.3 31.2 %all-to-all-start.3 = ((bf16[4,256,256]{2,1,0:T(8,128)(2,1)}), bf16[4,256,256]{2,1,0:T(8,128)(2,1)S(1)}, u32[]{:S(2)}, u32[]{:S(2)}) async-start(bf16[4,256,256]{2,1,0:T(8,128)(2,1)} %bitcast.162), calls=%async_computation.3 | async-start | bytes 1048576 | tf_op jit(solution)/shard_map/all_to_all | solution.py:286
  555.5 67.9 %collective-permute-start.4 = (bf16[2,256,256]{2,1,0:T(8,128)(2,1)}, bf16[2,256,256]{2,1,0:T(8,128)(2,1)}, u32[]{:S(2)}, u32[]{:S(2)}) collective-permute-start(bf16[2,256,256]{2,1,0:T(8,128)(2,1)} %constant_dynamic-slice_fusion.3), channel_id=1, source_target_pairs={{0,16},{16,0},{1,17},{17,1},{2,18},{18,2},{3,19},{19,3},{4,20},{20... | collective-permute-start | bytes 786440 | tf_op jit(solution)/shard_map/ppermute | solution.py:256
  583.3 40.1 %collective-permute-start.9 = (bf16[2,256,256]{2,1,0:T(8,128)(2,1)}, bf16[2,256,256]{2,1,0:T(8,128)(2,1)}, u32[]{:S(2)}, u32[]{:S(2)}) collective-permute-start(bf16[2,256,256]{2,1,0:T(8,128)(2,1)} %constant_dynamic-slice_fusion), channel_id=1, source_target_pairs={{0,16},{16,0},{1,17},{17,1},{2,18},{18,2},{3,19},{19,3},{4,20},{20... | collective-permute-start | bytes 786440 | tf_op jit(solution)/shard_map/ppermute | solution.py:256
  625.4 2.8 collective-permute-start.10
  627.6 3.3 collective-permute-start.11
  (42 other events, 275.7 us)
Sparse Core Ops, SparseCore 0:
  11.3 61.7 all-gather.7
  76.5 66.7 all-gather.5
  146.0 70.3 all-gather.11
  219.6 87.3 all-gather.9
  369.2 51.2 reduce-scatter.4
  423.5 88.4 reduce-scatter.8
  514.3 35.7 reduce-scatter.6
  552.3 50.4 reduce-scatter.10
